TPU v7x, 32 devices: a whole 2x2x4 slice. The times are simulated.
32 devices in a mesh: blk: 16 (over z, x, core), mp: 2 (over y).
Axes of the slice: x: 2, y: 2, z: 4, core: 2. Of those that a mesh axis runs over, the one named last changes fastest.
Arguments:
- features: bfloat16 [16, 2, 2, 256, 1280], P('blk', None, None, None, 'mp'), may hold values from -62 to 62
- w_query: bfloat16 [1280, 1280], P(None, 'mp'), may hold values from -2 to 2
- w_key: bfloat16 [1280, 1280], P(None, 'mp'), may hold values from -2 to 2
- w_value: bfloat16 [1280, 1280], P(None, 'mp'), may hold values from -0.15625 to 0.15625
- w_out: bfloat16 [1280, 1280], P('mp'), may hold values from -0.15625 to 0.15625
- w_head: bfloat16 [1280, 64], replicated, may hold values from -0.15625 to 0.15625
- offsets: int32 [16], P('blk'), may hold values from 0 to 255, as said below
- blend_mask: int32 [16, 64, 64], P('blk'), may hold values from 1 to 4
Outputs:
- panorama: float32 [2, 256, 256], P(None, 'blk')
Inputs may be any that keep to these rules, and one draw needn't show every extreme that they name: offsets[w] = 16 * w + s for one s shared by all windows, 0 <= s < 16.
All inputs are finite; a program needn't handle non-finite values.
Results may differ from a plain program's by a relative error of at most 0.0064.
Values may be sent and summed in bfloat16 or wider, within the bound.
No kernel may reach another device: no remote copies, remote signals or barrier semaphores. Data moves between devices by JAX's collectives and lax.ppermute only.
A program may use at most 64 MiB of HBM per device.

v0:
```python
import jax
import jax.numpy as jnp
from jax import lax
from jax.sharding import PartitionSpec as P

HEAD = 64
GRID = 16
PATCH = 4
CHAN = 4
STRIDE = 16
WINDOW = 64
OUTW = 64
guidance = 3.0


def shifted(x, axis, by):
    count = lax.axis_size(axis)
    return lax.ppermute(x, axis, [(i, (i + by) % count) for i in range(count)])


def shards(features, w_query, w_key, w_value, w_out, w_head, offsets, blend_mask):
    gathered = lax.all_gather(features, "mp", axis=4, tiled=True)
    batch_count = gathered.shape[1]
    token_count = gathered.shape[3]
    model_width = gathered.shape[4]
    sequences = batch_count * 2
    local_heads = w_query.shape[1] // HEAD
    token_plain = gathered.reshape(-1, model_width)
    token_rows = token_plain.astype(jnp.float32)
    row_mean = jnp.mean(token_rows, axis=1, keepdims=True)
    centred = token_rows - row_mean
    row_var = jnp.mean(centred * centred, axis=1, keepdims=True)
    normed = (centred * lax.rsqrt(row_var + 1e-05)).astype(jnp.bfloat16)
    queries = (
        jnp.dot(normed, w_query, preferred_element_type=jnp.float32)
        .astype(jnp.bfloat16)
        .reshape(sequences, token_count, local_heads, HEAD)
    )
    key_rows = (
        jnp.dot(normed, w_key, preferred_element_type=jnp.float32)
        .astype(jnp.bfloat16)
        .reshape(sequences, token_count, local_heads, HEAD)
    )
    value_rows = (
        jnp.dot(normed, w_value, preferred_element_type=jnp.float32)
        .astype(jnp.bfloat16)
        .reshape(sequences, token_count, local_heads, HEAD)
    )
    scores = (
        jnp.einsum("sqhd,skhd->shqk", queries, key_rows, preferred_element_type=jnp.float32)
        / HEAD**0.5
    )
    scores = scores - jnp.max(scores, axis=3, keepdims=True)
    expont = jnp.exp(scores)
    attend = (expont / jnp.sum(expont, axis=3, keepdims=True)).astype(jnp.bfloat16)
    context = jnp.einsum(
        "shqk,skhd->sqhd", attend, value_rows, preferred_element_type=jnp.float32
    ).astype(jnp.bfloat16)
    context = context.reshape(-1, local_heads * HEAD)
    partial_value = jnp.dot(context, w_out, preferred_element_type=jnp.float32)
    head_weight = w_head.astype(jnp.float32)
    head_part = jnp.dot(partial_value, head_weight, precision=lax.Precision.HIGHEST)
    tok_out = lax.psum(head_part.astype(jnp.bfloat16), "mp").astype(jnp.float32) + jnp.dot(
        token_plain, w_head, preferred_element_type=jnp.float32
    )
    tok_out = tok_out.reshape(batch_count, 2, token_count, OUTW)
    guided = tok_out[:, 0] + guidance * (tok_out[:, 1] - tok_out[:, 0])
    spread = guided.reshape(batch_count, GRID, GRID, PATCH, PATCH, CHAN).transpose(0, 2, 3, 1, 4, 5)
    spread = spread.reshape(batch_count, WINDOW, WINDOW * CHAN)
    weight = blend_mask[0].astype(jnp.float32)
    weighted = spread * jnp.repeat(weight, CHAN, axis=1)[None]
    shift_cols = offsets[0] - STRIDE * lax.axis_index("blk")
    zero_index = jnp.zeros((), jnp.int32)
    frame_num = lax.dynamic_update_slice(
        jnp.zeros((batch_count, WINDOW + STRIDE, WINDOW * CHAN), jnp.float32),
        weighted,
        (zero_index, shift_cols, zero_index),
    )
    frame_weight = lax.dynamic_update_slice(
        jnp.zeros((WINDOW + STRIDE, WINDOW), jnp.float32), weight, (shift_cols, zero_index)
    )
    piece_count = WINDOW // STRIDE + 1
    numerators = [frame_num[:, j * STRIDE : (j + 1) * STRIDE] for j in range(piece_count)]
    weight_pieces = [frame_weight[j * STRIDE : (j + 1) * STRIDE] for j in range(piece_count)]
    blended_num = numerators[0]
    blended_weight = weight_pieces[0]
    for j in range(1, piece_count):
        arrived = shifted((numerators[j], weight_pieces[j]), "blk", j)
        blended_num = blended_num + arrived[0]
        blended_weight = blended_weight + arrived[1]
    return blended_num / jnp.repeat(blended_weight, CHAN, axis=1)[None]


def solution(mesh):
    return jax.shard_map(
        shards,
        mesh=mesh,
        in_specs=(
            P("blk", None, None, None, "mp"),
            P(None, "mp"),
            P(None, "mp"),
            P(None, "mp"),
            P("mp", None),
            P(),
            P("blk"),
            P("blk", None, None),
        ),
        out_specs=P(None, "blk", None),
        check_vma=False,
    )
```

profile of v0, /device:TPU:0, one launch (start us, length us, event | category | flops | bytes accessed | tf_op | source)
XLA Modules:
  0.0 160.9 jit_solution(14204713652645674457)
XLA Ops:
  6.5 0.7 all-gather.2.cloned.1.call-update
  8.0 0.8 convert_bitcast_fusion
  8.8 0.4 dynamic_update_slice.7
  9.3 41.4 %all-gather.2.cloned.1.call-done = bf16[1,2,2,256,1280]{4,3,2,1,0:T(8,128)(2,1)} async-done(((bf16[1,2,2,256,640]{4,3,2,1,0:T(8,128)(2,1)}), bf16[1,2,2,256,1280]{4,3,2,1,0:T(8,128)(2,1)}) %all-gather.2.cloned.1.call-update) | async-done | bytes 2621456 | tf_op jit(solution)/shard_map/all_gather | solution.py:22
  50.6 2.3 %convert_reduce_fusion = f32[2,2,256]{2,1,0:T(2,128)S(1)} fusion(bf16[1,2,2,256,1280]{4,3,2,1,0:T(8,128)(2,1)} %all-gather.2.cloned.1.call-done), kind=kLoop, calls=%fused_computation.6 | loop fusion | flops 2620416 | bytes 2625536 | tf_op jit(solution)/shard_map/reduce_sum | solution.py:30
  53.0 0.2 copy-done.1
  53.2 0.8 fusion.5
  54.0 0.7 multiply_convert_fusion
  54.7 1.5 copy-done.2
  56.2 2.2 %convolution_convert_fusion = bf16[1024,640]{1,0:T(8,128)(2,1)S(1)} fusion(bf16[1024,1280]{1,0:T(8,128)(2,1)S(1)} %multiply_convert_fusion, bf16[1280,640]{1,0:T(8,128)(2,1)S(1)} %copy-done.6), kind=kOutput, calls=%fused_computation.13 | convolution fusion | flops 1678376960 | bytes 5570560 | tf_op jit(solution)/shard_map/dot_general | solution.py:40
  58.5 1.5 copy.35
  60.0 2.9 %reshape.66 = bf16[4,256,10,64]{1,0,3,2:T(4,128)(2,1)S(1)} reshape(bf16[1024,640]{0,1:T(8,128)(2,1)} %copy.35) | data formatting | bytes 2621440 | tf_op jit(solution)/shard_map/reshape | solution.py:42
  62.9 5.6 %convolution_convert_fusion.1 = bf16[1024,640]{1,0:T(8,128)(2,1)} fusion(bf16[1024,1280]{1,0:T(8,128)(2,1)} %copy-done.2, bf16[1280,640]{1,0:T(8,128)(2,1)} %param.9), kind=kOutput, calls=%fused_computation.14 | convolution fusion | flops 1678376960 | bytes 5570560 | tf_op jit(solution)/shard_map/dot_general | solution.py:35
  68.5 3.3 %convolution_convert_fusion.2 = bf16[1024,640]{1,0:T(8,128)(2,1)} fusion(bf16[1024,1280]{1,0:T(8,128)(2,1)S(1)} %copy-done.3, bf16[1280,640]{1,0:T(8,128)(2,1)S(1)} %copy-done.7), kind=kOutput, calls=%fused_computation.15 | convolution fusion | flops 1678376960 | bytes 5570560 | tf_op jit(solution)/shard_map/dot_general | solution.py:45
  71.8 2.5 %copy.33 = bf16[1024,640]{0,1:T(8,128)(2,1)} copy(bf16[1024,640]{1,0:T(8,128)(2,1)} %convolution_convert_fusion.2) | data formatting | bytes 2621440 | tf_op jit(solution)/shard_map/convert_element_type | solution.py:46
  74.3 3.8 %reshape.64 = bf16[4,256,10,64]{1,0,3,2:T(4,128)(2,1)} reshape(bf16[1024,640]{0,1:T(8,128)(2,1)} %copy.33) | data formatting | bytes 2621440 | tf_op jit(solution)/shard_map/reshape | solution.py:47
  78.0 2.5 %copy.34 = bf16[1024,640]{0,1:T(8,128)(2,1)} copy(bf16[1024,640]{1,0:T(8,128)(2,1)} %convolution_convert_fusion.1) | data formatting | bytes 2621440 | tf_op jit(solution)/shard_map/convert_element_type | solution.py:36
  80.5 3.8 %reshape.65 = bf16[4,256,10,64]{1,0,3,2:T(4,128)(2,1)} reshape(bf16[1024,640]{0,1:T(8,128)(2,1)} %copy.34) | data formatting | bytes 2621440 | tf_op jit(solution)/shard_map/reshape | solution.py:37
  84.3 2.9 %fusion.11 = f32[4,10,256,256]{2,3,1,0:T(8,128)S(1)} fusion(bf16[4,256,10,64]{1,0,3,2:T(4,128)(2,1)S(1)} %reshape.66, bf16[4,256,10,64]{1,0,3,2:T(4,128)(2,1)} %reshape.65), kind=kOutput, calls=%fused_computation.18 | convolution fusion | flops 335544320 | bytes 13107200 | tf_op jit(solution)/shard_map/sqhd,skhd->shqk/dot_general | solution.py:50
  87.2 5.4 %fusion.23 = (f32[4,10,256]{2,1,0:T(8,128)S(1)}, f32[4,10,256,256]{2,3,1,0:T(8,128)}) fusion(f32[4,10,256,256]{2,3,1,0:T(8,128)S(1)} %fusion.11), kind=kOutput, calls=%fused_computation.39 | output fusion | flops 10486015 | bytes 21012480 | tf_op jit(solution)/shard_map/sub | solution.py:53
  92.6 4.9 %fusion.9 = bf16[4,256,10,64]{1,3,2,0:T(8,128)(2,1)S(1)} fusion(f32[4,10,256,256]{2,3,1,0:T(8,128)} %get-tuple-element.19, f32[4,10,256]{2,1,0:T(8,128)S(1)} %get-tuple-element.18, bf16[4,256,10,64]{1,0,3,2:T(4,128)(2,1)S(1)} %copy-done.4), kind=kOutput, calls=%fused_computation.16 | convolution fusion | flops 341442560 | bytes 13148160 | tf_op jit(solution)/shard_map/shqk,skhd->sqhd/dot_general | solution.py:56
  97.5 1.0 copy.40
  98.6 0.3 copy.62
  98.9 2.3 %fusion.24 = f32[1024,1280]{1,0:T(8,128)S(1)} fusion(bf16[1024,640]{0,1:T(8,128)(2,1)S(1)} %bitcast.57, bf16[640,1280]{1,0:T(8,128)(2,1)S(1)} %copy-done), kind=kOutput, calls=%fused_computation.40 | convolution fusion | flops 1677721600 | bytes 8192000 | tf_op jit(solution)/shard_map/dot_general | solution.py:60
  101.2 3.5 %convolution_convert_fusion.3 = bf16[1024,64]{0,1:T(8,128)(2,1)} fusion(f32[1024,1280]{1,0:T(8,128)S(1)} %fusion.24, bf16[1280,64]{0,1:T(8,128)(2,1)S(1)} %copy-done.5), kind=kOutput, calls=%fused_computation.22 | convolution fusion | flops 1006698496 | bytes 5537792 | tf_op jit(solution)/shard_map/dot_general | solution.py:62
  104.7 0.1 fusion.22
  104.8 0.7 collective-permute-start.6
  105.6 0.9 collective-permute-start.4
  106.6 1.5 collective-permute-start.5
  108.0 1.5 collective-permute-start.7
  109.6 16.8 %all-reduce.2.cloned.1.call-done = bf16[1024,64]{0,1:T(8,128)(2,1)} async-done(((bf16[1024,64]{0,1:T(8,128)(2,1)}), bf16[1024,64]{0,1:T(8,128)(2,1)}) %all-reduce.2.cloned.1.call-update) | async-done | bytes 131088 | tf_op jit(solution)/shard_map/psum | solution.py:63
  126.3 2.6 %convolution_add_fusion = f32[1024,64]{0,1:T(8,128)S(1)} fusion(bf16[1024,1280]{1,0:T(8,128)(2,1)} %bitcast.55, bf16[1280,64]{0,1:T(8,128)(2,1)S(1)} %copy-done.5, bf16[1024,64]{0,1:T(8,128)(2,1)} %all-reduce.2.cloned.1.call-done), kind=kOutput, calls=%fused_computation.21 | convolution fusion | flops 167903232 | bytes 3178496 | tf_op jit(solution)/shard_map/dot_general | solution.py:63
  129.0 0.2 reshape.68
  129.2 0.2 fusion.20
  129.5 1.3 squeeze.11
  130.8 1.3 squeeze.12
  132.1 1.7 %add_bitcast_fusion = f32[2,16,4,16,4,4]{1,3,5,4,2,0:T(8,128)S(1)} fusion(f32[2,16,16,4,4,4]{2,1,5,4,3,0:T(8,128)} %squeeze.11, f32[2,16,16,4,4,4]{2,1,5,4,3,0:T(8,128)} %squeeze.12), kind=kLoop, calls=%fused_computation.23 | loop fusion | flops 98304 | bytes 393216 | tf_op jit(solution)/shard_map/transpose | solution.py:68
  133.8 4.7 %copy.43 = f32[2,16,4,16,4,4]{2,1,5,4,3,0:T(8,128)} copy(f32[2,16,4,16,4,4]{1,3,5,4,2,0:T(8,128)S(1)} %add_bitcast_fusion) | data formatting | bytes 262144 | tf_op jit(solution)/shard_map/transpose | solution.py:68
  138.6 3.6 %reshape.69 = f32[2,64,256]{1,2,0:T(8,128)S(1)} reshape(f32[2,16,4,16,4,4]{2,1,5,4,3,0:T(8,128)} %copy.43) | data formatting | bytes 262144 | tf_op jit(solution)/shard_map/reshape | solution.py:69
  142.3 0.1 copy.45
  142.4 0.4 dynamic_update_slice.6
  142.9 1.5 collective-permute-start.3
  144.5 2.3 %collective-permute-start.2 = (f32[2,16,256]{2,1,0:T(8,128)S(1)}, f32[2,16,256]{2,1,0:T(8,128)S(1)}, u32[]{:S(2)}, u32[]{:S(2)}) collective-permute-start(f32[2,16,256]{2,1,0:T(8,128)S(1)} %get-tuple-element.9), channel_id=1, source_target_pairs={{0,6},{2,8},{4,10},{6,12},{8,14},{10,16},{12,18},{14,20},{16,22},{... | collective-permute-start | bytes 98312 | tf_op jit(solution)/shard_map/ppermute | solution.py:18
  146.8 1.5 collective-permute-start.1
  148.5 0.5 collective-permute-done
  149.0 0.7 collective-permute-done.2
  149.6 3.8 %collective-permute-done.1 = f32[2,16,256]{2,1,0:T(8,128)S(1)} collective-permute-done((f32[2,16,256]{2,1,0:T(8,128)S(1)}, f32[2,16,256]{2,1,0:T(8,128)S(1)}, u32[]{:S(2)}, u32[]{:S(2)}) %collective-permute-start.1) | collective-permute-done | bytes 32800 | tf_op jit(solution)/shard_map/ppermute | solution.py:18
  153.4 0.6 fusion.17
  (44 shorter events, 0.8 us)
Async XLA Ops:
  6.5 92.3 %copy-start = (bf16[640,1280]{1,0:T(8,128)(2,1)S(1)}, bf16[640,1280]{1,0:T(8,128)(2,1)}, u32[]{:S(2)}) copy-start(bf16[640,1280]{1,0:T(8,128)(2,1)} %param.12) | copy-start | bytes 4915204
  6.5 44.1 %all-gather.2.cloned.1.call-start = ((), (), s32[]{:S(2)}) async-start(), calls=%async_computation | async-start | bytes 3932160 | tf_op jit(solution)/shard_map/all_gather | solution.py:22
  7.3 119.1 %all-reduce.2.cloned.1.call-start = ((), (), s32[]{:S(2)}) async-start(), calls=%async_computation.1 | async-start | bytes 262144 | tf_op jit(solution)/shard_map/psum | solution.py:63
  50.6 2.5 %copy-start.1 = (bf16[1,2,2,256,1280]{4,3,2,1,0:T(8,128)(2,1)S(1)}, bf16[1,2,2,256,1280]{4,3,2,1,0:T(8,128)(2,1)}, u32[]{:S(2)}) copy-start(bf16[1,2,2,256,1280]{4,3,2,1,0:T(8,128)(2,1)} %all-gather.2.cloned.1.call-done) | copy-start | bytes 7864324
  54.0 2.2 %copy-start.6 = (bf16[1280,640]{1,0:T(8,128)(2,1)S(1)}, bf16[1280,640]{1,0:T(8,128)(2,1)}, u32[]{:S(2)}) copy-start(bf16[1280,640]{1,0:T(8,128)(2,1)} %param.10) | copy-start | bytes 4915204
  54.7 1.5 copy-start.2
  62.8 5.6 %copy-start.3 = (bf16[1024,1280]{1,0:T(8,128)(2,1)S(1)}, bf16[1024,1280]{1,0:T(8,128)(2,1)}, u32[]{:S(2)}) copy-start(bf16[1024,1280]{1,0:T(8,128)(2,1)} %copy-done.2) | copy-start | bytes 7864324
  62.9 5.6 %copy-start.7 = (bf16[1280,640]{1,0:T(8,128)(2,1)S(1)}, bf16[1280,640]{1,0:T(8,128)(2,1)}, u32[]{:S(2)}) copy-start(bf16[1280,640]{1,0:T(8,128)(2,1)} %param.11) | copy-start | bytes 4915204
  87.2 5.5 %copy-start.4 = (bf16[4,256,10,64]{1,0,3,2:T(4,128)(2,1)S(1)}, bf16[4,256,10,64]{1,0,3,2:T(4,128)(2,1)}, u32[]{:S(2)}) copy-start(bf16[4,256,10,64]{1,0,3,2:T(4,128)(2,1)} %reshape.64) | copy-start | bytes 3932164
  98.9 2.3 %copy-start.5 = (bf16[1280,64]{0,1:T(8,128)(2,1)S(1)}, bf16[1280,64]{0,1:T(8,128)(2,1)}, u32[]{:S(2)}) copy-start(bf16[1280,64]{0,1:T(8,128)(2,1)} %param.13) | copy-start | bytes 491524
  104.8 38.1 %collective-permute-start.6 = (f32[16,64]{1,0:T(8,128)S(1)}, f32[16,64]{1,0:T(8,128)S(1)}, u32[]{:S(2)}, u32[]{:S(2)}) collective-permute-start(f32[16,64]{1,0:T(8,128)S(1)} %copy.59), channel_id=1, source_target_pairs={{0,6},{2,8},{4,10},{6,12},{8,14},{10,16},{12,18},{14,20},{16,22},{... | collective-permute-start | bytes 12296 | tf_op jit(solution)/shard_map/ppermute | solution.py:18
  105.6 38.8 %collective-permute-start.4 = (f32[16,64]{1,0:T(8,128)S(1)}, f32[16,64]{1,0:T(8,128)S(1)}, u32[]{:S(2)}, u32[]{:S(2)}) collective-permute-start(f32[16,64]{1,0:T(8,128)S(1)} %copy.57), channel_id=1, source_target_pairs={{0,2},{2,4},{4,6},{6,8},{8,10},{10,12},{12,14},{14,16},{16,18},{18... | collective-permute-start | bytes 12296 | tf_op jit(solution)/shard_map/ppermute | solution.py:18
  106.6 40.2 %collective-permute-start.5 = (f32[16,64]{1,0:T(8,128)S(1)}, f32[16,64]{1,0:T(8,128)S(1)}, u32[]{:S(2)}, u32[]{:S(2)}) collective-permute-start(f32[16,64]{1,0:T(8,128)S(1)} %copy.58), channel_id=1, source_target_pairs={{0,4},{2,6},{4,8},{6,10},{8,12},{10,14},{12,16},{14,18},{16,20},{1... | collective-permute-start | bytes 12296 | tf_op jit(solution)/shard_map/ppermute | solution.py:18
  108.0 40.3 %collective-permute-start.7 = (f32[16,64]{0,1:T(8,128)S(1)}, f32[16,64]{0,1:T(8,128)S(1)}, u32[]{:S(2)}, u32[]{:S(2)}) collective-permute-start(f32[16,64]{0,1:T(8,128)S(1)} %get-tuple-element.11), channel_id=1, source_target_pairs={{0,8},{2,10},{4,12},{6,14},{8,16},{10,18},{12,20},{14,22},{16,24},... | collective-permute-start | bytes 12296 | tf_op jit(solution)/shard_map/ppermute | solution.py:18
  142.9 6.1 %collective-permute-start = (f32[2,16,256]{2,1,0:T(8,128)S(1)}, f32[2,16,256]{2,1,0:T(8,128)S(1)}, u32[]{:S(2)}, u32[]{:S(2)}) collective-permute-start(f32[2,16,256]{2,1,0:T(8,128)S(1)} %get-tuple-element.7), channel_id=1, source_target_pairs={{0,2},{2,4},{4,6},{6,8},{8,10},{10,12},{12,14},{14,16},{16,18},{18... | collective-permute-start | bytes 98312 | tf_op jit(solution)/shard_map/ppermute | solution.py:18
  142.9 6.0 %collective-permute-start.3 = (f32[2,16,256]{2,1,0:T(8,128)S(1)}, f32[2,16,256]{2,1,0:T(8,128)S(1)}, u32[]{:S(2)}, u32[]{:S(2)}) collective-permute-start(f32[2,16,256]{2,1,0:T(8,128)S(1)} %get-tuple-element.8), channel_id=1, source_target_pairs={{0,8},{2,10},{4,12},{6,14},{8,16},{10,18},{12,20},{14,22},{16,24},... | collective-permute-start | bytes 98312 | tf_op jit(solution)/shard_map/ppermute | solution.py:18
  144.5 5.1 %collective-permute-start.2 = (f32[2,16,256]{2,1,0:T(8,128)S(1)}, f32[2,16,256]{2,1,0:T(8,128)S(1)}, u32[]{:S(2)}, u32[]{:S(2)}) collective-permute-start(f32[2,16,256]{2,1,0:T(8,128)S(1)} %get-tuple-element.9), channel_id=1, source_target_pairs={{0,6},{2,8},{4,10},{6,12},{8,14},{10,16},{12,18},{14,20},{16,22},{... | collective-permute-start | bytes 98312 | tf_op jit(solution)/shard_map/ppermute | solution.py:18
  146.8 6.6 %collective-permute-start.1 = (f32[2,16,256]{2,1,0:T(8,128)S(1)}, f32[2,16,256]{2,1,0:T(8,128)S(1)}, u32[]{:S(2)}, u32[]{:S(2)}) collective-permute-start(f32[2,16,256]{2,1,0:T(8,128)S(1)} %get-tuple-element.10), channel_id=1, source_target_pairs={{0,4},{2,6},{4,8},{6,10},{8,12},{10,14},{12,16},{14,18},{16,20},{1... | collective-permute-start | bytes 98312 | tf_op jit(solution)/shard_map/ppermute | solution.py:18
Sparse Core Ops, SparseCore 0:
  8.9 41.7 all-gather.1
  104.8 21.5 all-reduce.1
where the time goes:
time: 161 us
  waiting for transfers between devices  63.8 us (40%)
  local copies, waits for them, and re-layouts  33 us (20%)
  matrix products  27.3 us (17%)
  between operations  14.4 us (9%)
  other arithmetic  12.4 us (8%)
  starting transfers between devices  9.98 us (6%)
    all_gather x1, waiting for transfers between devices, shards(): gathered = lax.all_gather(features, 'mp', axis=4, tiled=True)  41.4 us
    psum x1, waiting for transfers between devices, shards(): lax.psum(head_part.astype(jnp.bfloat16), 'mp').astype(jnp.float32)  16.8 us
    ppermute x8, starting transfers between devices, shifted(): return lax.ppermute(x, axis, [(i, (i + by) % count) for i in range(count)])  9.94 us
    dot_general x1, matrix products, shards(): jnp.dot(normed, w_query, preferred_element_type=jnp.float32)  5.62 us
    sub x1, other arithmetic, shards(): scores = scores - jnp.max(scores, axis=3, keepdims=True)  5.44 us
    ppermute x8, waiting for transfers between devices, shifted(): return lax.ppermute(x, axis, [(i, (i + by) % count) for i in range(count)])  4.95 us
    dot_general x1, matrix products, shards(): jnp.einsum('shqk,skhd->sqhd', attend, value_rows, preferred_element_type=...  4.91 us
    transpose x1, local copies, waits for them, and re-layouts, shards(): guided.reshape(batch_count, GRID, GRID, PATCH, PATCH, CHAN)  4.74 us
  transfers between devices with their start and end apart: 10, of which 5 were waited for; matrix products, arithmetic and copies ran while one was open for 11% of the time, Pallas kernels for 0%

commit v1 on v0

--- a/solution.py
+++ b/solution.py
@@ -2,6 +2,7 @@
 import jax.numpy as jnp
 from jax import lax
 from jax.sharding import PartitionSpec as P
+from jax.lax import all_gather
 
 HEAD = 64
 GRID = 16
@@ -60,9 +61,9 @@
     partial_value = jnp.dot(context, w_out, preferred_element_type=jnp.float32)
     head_weight = w_head.astype(jnp.float32)
     head_part = jnp.dot(partial_value, head_weight, precision=lax.Precision.HIGHEST)
-    tok_out = lax.psum(head_part.astype(jnp.bfloat16), "mp").astype(jnp.float32) + jnp.dot(
-        token_plain, w_head, preferred_element_type=jnp.float32
-    )
+    tok_out = jnp.sum(all_gather(head_part.astype(jnp.bfloat16), axis_name="mp"), axis=0).astype(
+        jnp.float32
+    ) + jnp.dot(token_plain, w_head, preferred_element_type=jnp.float32)
     tok_out = tok_out.reshape(batch_count, 2, token_count, OUTW)
     guided = tok_out[:, 0] + guidance * (tok_out[:, 1] - tok_out[:, 0])
     spread = guided.reshape(batch_count, GRID, GRID, PATCH, PATCH, CHAN).transpose(0, 2, 3, 1, 4, 5)

time: 161 us -> 146 us (0.907)
  waiting for transfers between devices: 63.8 us -> 40.5 us
  blocking collectives: 0 us -> 5.73 us
  starting transfers between devices: 9.98 us -> 11.6 us
    psum x1 -> x0, waiting for transfers between devices: 16.8 us -> none  [shards(): lax.psum(head_part.astype(jnp.bfloat16), 'mp').astype(jnp.float32)]
    all_gather x1, waiting for transfers between devices: 41.4 us -> 34.8 us  [shards(): gathered = lax.all_gather(features, 'mp', axis=4, tiled=True)]
    all_gather x0 -> x1, blocking collectives: none -> 5.73 us  [shards(): all_gather(head_part.astype(jnp.bfloat16), axis_name='mp')]
    ppermute x8, starting transfers between devices: 9.94 us -> 11.6 us  [shifted(): return lax.ppermute(x, axis, [(i, (i + by) % count) for i in range(count)])]
  transfers between devices with their start and end apart: 10 -> 9, of which waited for: 5 -> 4; matrix products, arithmetic and copies ran while one was open for 11% -> 49% of each run, Pallas kernels for 0% -> 0%
where the time goes in v1:
time: 146 us; the launch traced here: 145 us
  waiting for transfers between devices  40.5 us (28%)
  local copies, waits for them, and re-layouts  33.2 us (23%)
  matrix products  26.6 us (18%)
  between operations  14.4 us (10%)
  other arithmetic  13.1 us (9%)
  starting transfers between devices  11.6 us (8%)
  blocking collectives  5.73 us (4%)
    all_gather x1, waiting for transfers between devices, shards(): gathered = lax.all_gather(features, 'mp', axis=4, tiled=True)  34.8 us
    ppermute x8, starting transfers between devices, shifted(): return lax.ppermute(x, axis, [(i, (i + by) % count) for i in range(count)])  11.6 us
    all_gather x1, blocking collectives, shards(): all_gather(head_part.astype(jnp.bfloat16), axis_name='mp')  5.73 us
    dot_general x1, matrix products, shards(): jnp.dot(normed, w_query, preferred_element_type=jnp.float32)  5.63 us
    sub x1, other arithmetic, shards(): scores = scores - jnp.max(scores, axis=3, keepdims=True)  5.43 us
    ppermute x8, waiting for transfers between devices, shifted(): return lax.ppermute(x, axis, [(i, (i + by) % count) for i in range(count)])  4.96 us
    dot_general x1, matrix products, shards(): jnp.einsum('shqk,skhd->sqhd', attend, value_rows, preferred_element_type=...  4.91 us
    transpose x1, local copies, waits for them, and re-layouts, shards(): guided.reshape(batch_count, GRID, GRID, PATCH, PATCH, CHAN)  4.52 us
  transfers between devices with their start and end apart: 9, of which 4 were waited for; matrix products, arithmetic and copies ran while one was open for 49% of the time, Pallas kernels for 0%

profile of v1, /device:TPU:0, one launch (start us, length us, event | category | flops | bytes accessed | tf_op | source)
XLA Modules:
  0.0 145.1 jit_solution(3996643897503651142)
XLA Ops:
  6.5 0.7 all-gather.3.cloned.1.call-update
  7.9 0.8 convert_bitcast_fusion
  8.8 0.4 dynamic_update_slice.7
  9.4 2.4 %collective-permute-start.6 = (f32[16,64]{1,0:T(8,128)S(1)}, f32[16,64]{1,0:T(8,128)S(1)}, u32[]{:S(2)}, u32[]{:S(2)}) collective-permute-start(f32[16,64]{1,0:T(8,128)S(1)} %copy.59), channel_id=1, source_target_pairs={{0,6},{2,8},{4,10},{6,12},{8,14},{10,16},{12,18},{14,20},{16,22},{... | collective-permute-start | bytes 12296 | tf_op jit(solution)/shard_map/ppermute | solution.py:19
  11.9 0.8 collective-permute-start.4
  12.7 1.5 %collective-permute-start.5 = (f32[16,64]{1,0:T(8,128)S(1)}, f32[16,64]{1,0:T(8,128)S(1)}, u32[]{:S(2)}, u32[]{:S(2)}) collective-permute-start(f32[16,64]{1,0:T(8,128)S(1)} %copy.58), channel_id=1, source_target_pairs={{0,4},{2,6},{4,8},{6,10},{8,12},{10,14},{12,16},{14,18},{16,20},{1... | collective-permute-start | bytes 12296 | tf_op jit(solution)/shard_map/ppermute | solution.py:19
  14.2 1.6 %collective-permute-start.7 = (f32[16,64]{0,1:T(8,128)S(1)}, f32[16,64]{0,1:T(8,128)S(1)}, u32[]{:S(2)}, u32[]{:S(2)}) collective-permute-start(f32[16,64]{0,1:T(8,128)S(1)} %get-tuple-element.11), channel_id=1, source_target_pairs={{0,8},{2,10},{4,12},{6,14},{8,16},{10,18},{12,20},{14,22},{16,24},... | collective-permute-start | bytes 12296 | tf_op jit(solution)/shard_map/ppermute | solution.py:19
  15.8 34.8 %all-gather.3.cloned.1.call-done = bf16[1,2,2,256,1280]{4,3,2,1,0:T(8,128)(2,1)} async-done(((bf16[1,2,2,256,640]{4,3,2,1,0:T(8,128)(2,1)}), bf16[1,2,2,256,1280]{4,3,2,1,0:T(8,128)(2,1)}) %all-gather.3.cloned.1.call-update) | async-done | bytes 2621456 | tf_op jit(solution)/shard_map/all_gather | solution.py:23
  50.6 2.3 %convert_reduce_fusion = f32[2,2,256]{2,1,0:T(2,128)S(1)} fusion(bf16[1,2,2,256,1280]{4,3,2,1,0:T(8,128)(2,1)} %all-gather.3.cloned.1.call-done), kind=kLoop, calls=%fused_computation.6 | loop fusion | flops 2620416 | bytes 2625536 | tf_op jit(solution)/shard_map/reduce_sum | solution.py:31
  53.0 0.2 copy-done.1
  53.2 0.8 fusion.5
  54.0 0.7 multiply_convert_fusion
  54.7 1.5 %copy-done.2 = bf16[1024,1280]{1,0:T(8,128)(2,1)} copy-done((bf16[1024,1280]{1,0:T(8,128)(2,1)}, bf16[1024,1280]{1,0:T(8,128)(2,1)S(1)}, u32[]{:S(2)}) %copy-start.2) | copy-done | bytes 2621464
  56.2 2.2 %convolution_convert_fusion = bf16[1024,640]{1,0:T(8,128)(2,1)S(1)} fusion(bf16[1024,1280]{1,0:T(8,128)(2,1)S(1)} %multiply_convert_fusion, bf16[1280,640]{1,0:T(8,128)(2,1)S(1)} %copy-done.6), kind=kOutput, calls=%fused_computation.13 | convolution fusion | flops 1678376960 | bytes 5570560 | tf_op jit(solution)/shard_map/dot_general | solution.py:41
  58.5 1.7 %copy.35 = bf16[1024,640]{0,1:T(8,128)(2,1)} copy(bf16[1024,640]{1,0:T(8,128)(2,1)S(1)} %convolution_convert_fusion) | data formatting | bytes 2621440 | tf_op jit(solution)/shard_map/convert_element_type | solution.py:42
  60.1 2.9 %reshape.66 = bf16[4,256,10,64]{1,0,3,2:T(4,128)(2,1)S(1)} reshape(bf16[1024,640]{0,1:T(8,128)(2,1)} %copy.35) | data formatting | bytes 2621440 | tf_op jit(solution)/shard_map/reshape | solution.py:43
  63.1 5.6 %convolution_convert_fusion.1 = bf16[1024,640]{1,0:T(8,128)(2,1)} fusion(bf16[1024,1280]{1,0:T(8,128)(2,1)} %copy-done.2, bf16[1280,640]{1,0:T(8,128)(2,1)} %param.9), kind=kOutput, calls=%fused_computation.14 | convolution fusion | flops 1678376960 | bytes 5570560 | tf_op jit(solution)/shard_map/dot_general | solution.py:36
  68.7 3.3 %convolution_convert_fusion.2 = bf16[1024,640]{1,0:T(8,128)(2,1)} fusion(bf16[1024,1280]{1,0:T(8,128)(2,1)S(1)} %copy-done.3, bf16[1280,640]{1,0:T(8,128)(2,1)S(1)} %copy-done.7), kind=kOutput, calls=%fused_computation.15 | convolution fusion | flops 1678376960 | bytes 5570560 | tf_op jit(solution)/shard_map/dot_general | solution.py:46
  72.0 2.5 %copy.33 = bf16[1024,640]{0,1:T(8,128)(2,1)} copy(bf16[1024,640]{1,0:T(8,128)(2,1)} %convolution_convert_fusion.2) | data formatting | bytes 2621440 | tf_op jit(solution)/shard_map/convert_element_type | solution.py:47
  74.4 3.8 %reshape.64 = bf16[4,256,10,64]{1,0,3,2:T(4,128)(2,1)} reshape(bf16[1024,640]{0,1:T(8,128)(2,1)} %copy.33) | data formatting | bytes 2621440 | tf_op jit(solution)/shard_map/reshape | solution.py:48
  78.2 2.5 %copy.34 = bf16[1024,640]{0,1:T(8,128)(2,1)} copy(bf16[1024,640]{1,0:T(8,128)(2,1)} %convolution_convert_fusion.1) | data formatting | bytes 2621440 | tf_op jit(solution)/shard_map/convert_element_type | solution.py:37
  80.7 3.8 %reshape.65 = bf16[4,256,10,64]{1,0,3,2:T(4,128)(2,1)} reshape(bf16[1024,640]{0,1:T(8,128)(2,1)} %copy.34) | data formatting | bytes 2621440 | tf_op jit(solution)/shard_map/reshape | solution.py:38
  84.5 2.9 %fusion.11 = f32[4,10,256,256]{2,3,1,0:T(8,128)S(1)} fusion(bf16[4,256,10,64]{1,0,3,2:T(4,128)(2,1)S(1)} %reshape.66, bf16[4,256,10,64]{1,0,3,2:T(4,128)(2,1)} %reshape.65), kind=kOutput, calls=%fused_computation.18 | convolution fusion | flops 335544320 | bytes 13107200 | tf_op jit(solution)/shard_map/sqhd,skhd->shqk/dot_general | solution.py:51
  87.3 5.4 %fusion.23 = (f32[4,10,256]{2,1,0:T(8,128)S(1)}, f32[4,10,256,256]{2,3,1,0:T(8,128)}) fusion(f32[4,10,256,256]{2,3,1,0:T(8,128)S(1)} %fusion.11), kind=kOutput, calls=%fused_computation.39 | output fusion | flops 10486015 | bytes 21012480 | tf_op jit(solution)/shard_map/sub | solution.py:54
  92.8 4.9 %fusion.9 = bf16[4,256,10,64]{1,3,2,0:T(8,128)(2,1)S(1)} fusion(f32[4,10,256,256]{2,3,1,0:T(8,128)} %get-tuple-element.19, f32[4,10,256]{2,1,0:T(8,128)S(1)} %get-tuple-element.18, bf16[4,256,10,64]{1,0,3,2:T(4,128)(2,1)S(1)} %copy-done.4), kind=kOutput, calls=%fused_computation.16 | convolution fusion | flops 341442560 | bytes 13148160 | tf_op jit(solution)/shard_map/shqk,skhd->sqhd/dot_general | solution.py:57
  97.7 1.0 copy.40
  98.7 0.3 copy.62
  99.0 2.3 %fusion.24 = f32[1024,1280]{1,0:T(8,128)S(1)} fusion(bf16[1024,640]{0,1:T(8,128)(2,1)S(1)} %bitcast.59, bf16[640,1280]{1,0:T(8,128)(2,1)S(1)} %copy-done), kind=kOutput, calls=%fused_computation.40 | convolution fusion | flops 1677721600 | bytes 8192000 | tf_op jit(solution)/shard_map/dot_general | solution.py:61
  101.3 2.8 %convolution_convert_fusion.3 = bf16[1024,64]{0,1:T(8,128)(2,1)S(1)} fusion(f32[1024,1280]{1,0:T(8,128)S(1)} %fusion.24, bf16[1280,64]{0,1:T(8,128)(2,1)S(1)} %copy-done.5), kind=kOutput, calls=%fused_computation.22 | convolution fusion | flops 1006698496 | bytes 5537792 | tf_op jit(solution)/shard_map/dot_general | solution.py:63
  104.2 5.7 %all-gather = bf16[2048,64]{0,1:T(8,128)(2,1)S(1)} all-gather(bf16[1024,64]{0,1:T(8,128)(2,1)S(1)} %convolution_convert_fusion.3), channel_id=2, replica_groups=mesh['blk'=16,'mp'=2] {'mp'}, dimensions={0}, use_global_device_ids=true | all-gather | bytes 393216 | tf_op jit(solution)/shard_map/all_gather | solution.py:64
  109.9 0.2 reshape.70
  110.1 0.7 reduce_sum.42
  110.8 2.6 %convolution_add_fusion = f32[1024,64]{0,1:T(8,128)S(1)} fusion(bf16[1024,1280]{1,0:T(8,128)(2,1)} %bitcast.57, bf16[1280,64]{0,1:T(8,128)(2,1)S(1)} %copy-done.5, bf16[1024,64]{0,1:T(8,128)(2,1)S(1)} %reduce_sum.42), kind=kOutput, calls=%fused_computation.21 | convolution fusion | flops 167903232 | bytes 3178496 | tf_op jit(solution)/shard_map/dot_general | solution.py:66
  113.4 0.2 reshape.68
  113.6 0.2 fusion.20
  113.9 1.3 squeeze.11
  115.2 1.3 squeeze.12
  116.5 1.7 %add_bitcast_fusion = f32[2,16,4,16,4,4]{1,3,5,4,2,0:T(8,128)S(1)} fusion(f32[2,16,16,4,4,4]{2,1,5,4,3,0:T(8,128)} %squeeze.11, f32[2,16,16,4,4,4]{2,1,5,4,3,0:T(8,128)} %squeeze.12), kind=kLoop, calls=%fused_computation.23 | loop fusion | flops 98304 | bytes 393216 | tf_op jit(solution)/shard_map/transpose | solution.py:69
  118.2 4.5 %copy.43 = f32[2,16,4,16,4,4]{2,1,5,4,3,0:T(8,128)} copy(f32[2,16,4,16,4,4]{1,3,5,4,2,0:T(8,128)S(1)} %add_bitcast_fusion) | data formatting | bytes 262144 | tf_op jit(solution)/shard_map/transpose | solution.py:69
  122.8 3.6 %reshape.69 = f32[2,64,256]{1,2,0:T(8,128)S(1)} reshape(f32[2,16,4,16,4,4]{2,1,5,4,3,0:T(8,128)} %copy.43) | data formatting | bytes 262144 | tf_op jit(solution)/shard_map/reshape | solution.py:70
  126.6 0.4 dynamic_update_slice.6
  127.1 1.5 %collective-permute-start.3 = (f32[2,16,256]{2,1,0:T(8,128)S(1)}, f32[2,16,256]{2,1,0:T(8,128)S(1)}, u32[]{:S(2)}, u32[]{:S(2)}) collective-permute-start(f32[2,16,256]{2,1,0:T(8,128)S(1)} %get-tuple-element.8), channel_id=1, source_target_pairs={{0,8},{2,10},{4,12},{6,14},{8,16},{10,18},{12,20},{14,22},{16,24},... | collective-permute-start | bytes 98312 | tf_op jit(solution)/shard_map/ppermute | solution.py:19
  128.7 2.3 %collective-permute-start.2 = (f32[2,16,256]{2,1,0:T(8,128)S(1)}, f32[2,16,256]{2,1,0:T(8,128)S(1)}, u32[]{:S(2)}, u32[]{:S(2)}) collective-permute-start(f32[2,16,256]{2,1,0:T(8,128)S(1)} %get-tuple-element.9), channel_id=1, source_target_pairs={{0,6},{2,8},{4,10},{6,12},{8,14},{10,16},{12,18},{14,20},{16,22},{... | collective-permute-start | bytes 98312 | tf_op jit(solution)/shard_map/ppermute | solution.py:19
  131.0 1.5 %collective-permute-start.1 = (f32[2,16,256]{2,1,0:T(8,128)S(1)}, f32[2,16,256]{2,1,0:T(8,128)S(1)}, u32[]{:S(2)}, u32[]{:S(2)}) collective-permute-start(f32[2,16,256]{2,1,0:T(8,128)S(1)} %get-tuple-element.10), channel_id=1, source_target_pairs={{0,4},{2,6},{4,8},{6,10},{8,12},{10,14},{12,16},{14,18},{16,20},{1... | collective-permute-start | bytes 98312 | tf_op jit(solution)/shard_map/ppermute | solution.py:19
  132.7 0.5 collective-permute-done
  133.2 0.7 collective-permute-done.2
  133.8 3.8 %collective-permute-done.1 = f32[2,16,256]{2,1,0:T(8,128)S(1)} collective-permute-done((f32[2,16,256]{2,1,0:T(8,128)S(1)}, f32[2,16,256]{2,1,0:T(8,128)S(1)}, u32[]{:S(2)}, u32[]{:S(2)}) %collective-permute-start.1) | collective-permute-done | bytes 32800 | tf_op jit(solution)/shard_map/ppermute | solution.py:19
  137.6 0.6 fusion.17
  (44 shorter events, 1.0 us)
Async XLA Ops:
  6.5 92.5 %copy-start = (bf16[640,1280]{1,0:T(8,128)(2,1)S(1)}, bf16[640,1280]{1,0:T(8,128)(2,1)}, u32[]{:S(2)}) copy-start(bf16[640,1280]{1,0:T(8,128)(2,1)} %param.12) | copy-start | bytes 4915204
  6.5 44.1 %all-gather.3.cloned.1.call-start = ((), (), s32[]{:S(2)}) async-start(), calls=%async_computation | async-start | bytes 3932160 | tf_op jit(solution)/shard_map/all_gather | solution.py:23
  9.4 117.8 %collective-permute-start.6 = (f32[16,64]{1,0:T(8,128)S(1)}, f32[16,64]{1,0:T(8,128)S(1)}, u32[]{:S(2)}, u32[]{:S(2)}) collective-permute-start(f32[16,64]{1,0:T(8,128)S(1)} %copy.59), channel_id=1, source_target_pairs={{0,6},{2,8},{4,10},{6,12},{8,14},{10,16},{12,18},{14,20},{16,22},{... | collective-permute-start | bytes 12296 | tf_op jit(solution)/shard_map/ppermute | solution.py:19
  11.9 116.8 %collective-permute-start.4 = (f32[16,64]{1,0:T(8,128)S(1)}, f32[16,64]{1,0:T(8,128)S(1)}, u32[]{:S(2)}, u32[]{:S(2)}) collective-permute-start(f32[16,64]{1,0:T(8,128)S(1)} %copy.57), channel_id=1, source_target_pairs={{0,2},{2,4},{4,6},{6,8},{8,10},{10,12},{12,14},{14,16},{16,18},{18... | collective-permute-start | bytes 12296 | tf_op jit(solution)/shard_map/ppermute | solution.py:19
  12.7 118.3 %collective-permute-start.5 = (f32[16,64]{1,0:T(8,128)S(1)}, f32[16,64]{1,0:T(8,128)S(1)}, u32[]{:S(2)}, u32[]{:S(2)}) collective-permute-start(f32[16,64]{1,0:T(8,128)S(1)} %copy.58), channel_id=1, source_target_pairs={{0,4},{2,6},{4,8},{6,10},{8,12},{10,14},{12,16},{14,18},{16,20},{1... | collective-permute-start | bytes 12296 | tf_op jit(solution)/shard_map/ppermute | solution.py:19
  14.2 118.4 %collective-permute-start.7 = (f32[16,64]{0,1:T(8,128)S(1)}, f32[16,64]{0,1:T(8,128)S(1)}, u32[]{:S(2)}, u32[]{:S(2)}) collective-permute-start(f32[16,64]{0,1:T(8,128)S(1)} %get-tuple-element.11), channel_id=1, source_target_pairs={{0,8},{2,10},{4,12},{6,14},{8,16},{10,18},{12,20},{14,22},{16,24},... | collective-permute-start | bytes 12296 | tf_op jit(solution)/shard_map/ppermute | solution.py:19
  50.6 2.5 %copy-start.1 = (bf16[1,2,2,256,1280]{4,3,2,1,0:T(8,128)(2,1)S(1)}, bf16[1,2,2,256,1280]{4,3,2,1,0:T(8,128)(2,1)}, u32[]{:S(2)}) copy-start(bf16[1,2,2,256,1280]{4,3,2,1,0:T(8,128)(2,1)} %all-gather.3.cloned.1.call-done) | copy-start | bytes 7864324
  54.0 2.2 %copy-start.6 = (bf16[1280,640]{1,0:T(8,128)(2,1)S(1)}, bf16[1280,640]{1,0:T(8,128)(2,1)}, u32[]{:S(2)}) copy-start(bf16[1280,640]{1,0:T(8,128)(2,1)} %param.10) | copy-start | bytes 4915204
  54.7 1.5 %copy-start.2 = (bf16[1024,1280]{1,0:T(8,128)(2,1)}, bf16[1024,1280]{1,0:T(8,128)(2,1)S(1)}, u32[]{:S(2)}) copy-start(bf16[1024,1280]{1,0:T(8,128)(2,1)S(1)} %multiply_convert_fusion) | copy-start | bytes 7864324
  63.0 5.7 %copy-start.3 = (bf16[1024,1280]{1,0:T(8,128)(2,1)S(1)}, bf16[1024,1280]{1,0:T(8,128)(2,1)}, u32[]{:S(2)}) copy-start(bf16[1024,1280]{1,0:T(8,128)(2,1)} %copy-done.2) | copy-start | bytes 7864324
  63.0 5.6 %copy-start.7 = (bf16[1280,640]{1,0:T(8,128)(2,1)S(1)}, bf16[1280,640]{1,0:T(8,128)(2,1)}, u32[]{:S(2)}) copy-start(bf16[1280,640]{1,0:T(8,128)(2,1)} %param.11) | copy-start | bytes 4915204
  87.3 5.4 %copy-start.4 = (bf16[4,256,10,64]{1,0,3,2:T(4,128)(2,1)S(1)}, bf16[4,256,10,64]{1,0,3,2:T(4,128)(2,1)}, u32[]{:S(2)}) copy-start(bf16[4,256,10,64]{1,0,3,2:T(4,128)(2,1)} %reshape.64) | copy-start | bytes 3932164
  99.0 2.3 %copy-start.5 = (bf16[1280,64]{0,1:T(8,128)(2,1)S(1)}, bf16[1280,64]{0,1:T(8,128)(2,1)}, u32[]{:S(2)}) copy-start(bf16[1280,64]{0,1:T(8,128)(2,1)} %param.13) | copy-start | bytes 491524
  127.1 6.1 %collective-permute-start = (f32[2,16,256]{2,1,0:T(8,128)S(1)}, f32[2,16,256]{2,1,0:T(8,128)S(1)}, u32[]{:S(2)}, u32[]{:S(2)}) collective-permute-start(f32[2,16,256]{2,1,0:T(8,128)S(1)} %get-tuple-element.7), channel_id=1, source_target_pairs={{0,2},{2,4},{4,6},{6,8},{8,10},{10,12},{12,14},{14,16},{16,18},{18... | collective-permute-start | bytes 98312 | tf_op jit(solution)/shard_map/ppermute | solution.py:19
  127.1 6.0 %collective-permute-start.3 = (f32[2,16,256]{2,1,0:T(8,128)S(1)}, f32[2,16,256]{2,1,0:T(8,128)S(1)}, u32[]{:S(2)}, u32[]{:S(2)}) collective-permute-start(f32[2,16,256]{2,1,0:T(8,128)S(1)} %get-tuple-element.8), channel_id=1, source_target_pairs={{0,8},{2,10},{4,12},{6,14},{8,16},{10,18},{12,20},{14,22},{16,24},... | collective-permute-start | bytes 98312 | tf_op jit(solution)/shard_map/ppermute | solution.py:19
  128.7 5.1 %collective-permute-start.2 = (f32[2,16,256]{2,1,0:T(8,128)S(1)}, f32[2,16,256]{2,1,0:T(8,128)S(1)}, u32[]{:S(2)}, u32[]{:S(2)}) collective-permute-start(f32[2,16,256]{2,1,0:T(8,128)S(1)} %get-tuple-element.9), channel_id=1, source_target_pairs={{0,6},{2,8},{4,10},{6,12},{8,14},{10,16},{12,18},{14,20},{16,22},{... | collective-permute-start | bytes 98312 | tf_op jit(solution)/shard_map/ppermute | solution.py:19
  131.0 6.6 %collective-permute-start.1 = (f32[2,16,256]{2,1,0:T(8,128)S(1)}, f32[2,16,256]{2,1,0:T(8,128)S(1)}, u32[]{:S(2)}, u32[]{:S(2)}) collective-permute-start(f32[2,16,256]{2,1,0:T(8,128)S(1)} %get-tuple-element.10), channel_id=1, source_target_pairs={{0,4},{2,6},{4,8},{6,10},{8,12},{10,14},{12,16},{14,18},{16,20},{1... | collective-permute-start | bytes 98312 | tf_op jit(solution)/shard_map/ppermute | solution.py:19
Sparse Core Ops, SparseCore 0:
  8.9 41.7 all-gather.2
